TPU v7x, 32 devices: a whole 2x2x4 slice. The times are simulated.
32 devices in a mesh: tensor: 2 (over x), expert: 8 (over z, y), replica: 2 (over core).
Axes of the slice: x: 2, y: 2, z: 4, core: 2. Of those that a mesh axis runs over, the one named last changes fastest.
Arguments:
- tokens: bfloat16 [6304, 768], P(('expert', 'replica')), may hold values from -6 to 6
- gains: float32 [2, 2, 768], replicated, may hold values from 0.5 to 1.5
- attn_qkv: bfloat16 [2, 3, 768, 768], P(None, None, None, 'tensor'), may hold values from -0.21875 to 0.21875
- attn_out: bfloat16 [2, 768, 768], P(None, 'tensor'), may hold values from -3 to 3
- router: bfloat16 [2, 768, 8], replicated, may hold values from -0.15625 to 0.15625
- expert_in: bfloat16 [2, 8, 768, 3072], P(None, 'expert', None, 'tensor'), may hold values from -0.21875 to 0.21875
- expert_out: bfloat16 [2, 8, 3072, 768], P(None, 'expert', 'tensor'), may hold values from -1.75 to 1.75
- routes: int32 [2, 6304, 2], P(None, ('expert', 'replica')), may hold values from 0 to 7, all different within a row; in each aligned block of 394 rows (0 to 393, 394 to 787, ..., all dimensions but the last counted through in order) at most 128 rows name the same one
- cotangent: bfloat16 [6304, 768], P(('expert', 'replica')), may hold values from -6 to 6
Outputs:
- mixed_out: bfloat16 [6304, 768], P(('expert', 'replica'))
- grad_tokens: float32 [6304, 768], P(('expert', 'replica'))
- grad_gains: float32 [2, 2, 768], replicated
- grad_attn_qkv: float32 [2, 3, 768, 768], P(None, None, None, 'tensor')
- grad_attn_out: float32 [2, 768, 768], P(None, 'tensor')
- grad_router: float32 [2, 768, 8], replicated
- grad_expert_in: float32 [2, 8, 768, 3072], P(None, 'expert', 'replica', 'tensor')
- grad_expert_out: float32 [2, 8, 3072, 768], P(None, 'expert', 'tensor', 'replica')
Inputs may be any that keep to these rules, and one draw needn't show every extreme that they name: In the tokens of one block of 394, no expert is named by more than 128 routes, and in every draw some expert by exactly 128; the two experts of a token differ.
All inputs are finite; a program needn't handle non-finite values.
Results may differ from a plain program's by a relative error of at most 0.02.
Values may be sent and summed in bfloat16 or wider, within the bound.
No kernel may reach another device: no remote copies, remote signals or barrier semaphores. Data moves between devices by JAX's collectives and lax.ppermute only.
A program may use at most 192 MiB of HBM per device.

v0:
```python
import jax
import jax.numpy as jnp
from jax import lax
from jax.sharding import PartitionSpec as P

HEAD_DIM = 64
SEQ = 197
EPSILON = 1e-06


def layer_norm(stream, gain):
    center = jnp.mean(stream, axis=-1, keepdims=True)
    shifted = stream - center
    spread = jnp.mean(shifted * shifted, axis=-1, keepdims=True)
    return shifted * lax.rsqrt(spread + EPSILON) * gain


def slot_index(route_ids, expert_count, capacity):
    labels = lax.broadcasted_iota(jnp.int32, (1, 1, expert_count), 2)
    route_hits = jnp.sum((route_ids[:, :, None] == labels).astype(jnp.int32), axis=1)
    before = jnp.cumsum(route_hits, axis=0) - route_hits
    return route_ids * capacity + jnp.take_along_axis(before, route_ids, axis=1)


def on_device(tokens, gains, attn_qkv, attn_out, router, expert_in, expert_out, routes, cotangent):
    row_count, model_width = tokens.shape
    layer_count = attn_qkv.shape[0]
    local_width = attn_qkv.shape[3]
    local_heads = local_width // HEAD_DIM
    image_count = row_count // SEQ
    expert_count = router.shape[2]
    capacity = 8 * (5 * row_count // (16 * expert_count) + 1)
    score_scale = HEAD_DIM ** (-0.5)
    residual = tokens.astype(jnp.float32)
    saved = []
    for layer_index in range(layer_count):
        normed, norm_pull = jax.vjp(layer_norm, residual, gains[layer_index, 0])
        normed_bf = normed.astype(jnp.bfloat16)
        projected = jnp.einsum(
            "td,cdf->ctf", normed_bf, attn_qkv[layer_index], preferred_element_type=jnp.float32
        ).astype(jnp.bfloat16)
        head_view = projected.reshape(3, image_count, SEQ, local_heads, HEAD_DIM)
        scores = (
            jnp.einsum(
                "bqhe,bkhe->bhqk", head_view[0], head_view[1], preferred_element_type=jnp.float32
            )
            * score_scale
        )
        row_max = jnp.max(scores, axis=-1, keepdims=True)
        exp_scores = jnp.exp(scores - row_max)
        exp_total = jnp.sum(exp_scores, axis=-1, keepdims=True)
        log_total = row_max + jnp.log(exp_total)
        attn_probs = (exp_scores / exp_total).astype(jnp.bfloat16)
        mixed_rows = jnp.einsum(
            "bhqk,bkhe->bqhe", attn_probs, head_view[2], preferred_element_type=jnp.float32
        )
        mixed_rows = mixed_rows.reshape(row_count, local_width).astype(jnp.bfloat16)
        attn_part = jnp.dot(mixed_rows, attn_out[layer_index], preferred_element_type=jnp.float32)
        residual = residual + lax.psum(attn_part, "tensor")
        moe_in, moe_pull = jax.vjp(layer_norm, residual, gains[layer_index, 1])
        moe_bf = moe_in.astype(jnp.bfloat16)
        gate_probs = jax.nn.softmax(
            jnp.dot(moe_bf, router[layer_index], preferred_element_type=jnp.float32), axis=-1
        )
        route_ids = routes[layer_index]
        slot_rows = slot_index(route_ids, expert_count, capacity).reshape(-1)
        picked = jnp.take_along_axis(gate_probs, route_ids, axis=1)
        send_buffer = jnp.zeros((expert_count * capacity, model_width), jnp.bfloat16)
        send_buffer = (
            send_buffer.at[slot_rows]
            .set(jnp.repeat(moe_bf, 2, axis=0))
            .reshape(expert_count, capacity, model_width)
        )
        received = lax.all_to_all(send_buffer, "expert", split_axis=0, concat_axis=0, tiled=True)
        source_count = received.shape[0]
        flat_in = received.reshape(-1, model_width)
        pre_act = jnp.dot(flat_in, expert_in[layer_index, 0], preferred_element_type=jnp.float32)
        activation = jax.nn.gelu(pre_act).astype(jnp.bfloat16)
        expert_part = jnp.dot(
            activation, expert_out[layer_index, 0], preferred_element_type=jnp.float32
        )
        expert_part = expert_part.reshape(source_count, capacity, model_width)
        returned = lax.all_to_all(expert_part, "expert", split_axis=0, concat_axis=0, tiled=True)
        chosen = returned.reshape(-1, model_width)[slot_rows].reshape(row_count, 2, model_width)
        moe_part = jnp.sum(picked[:, :, None] * chosen, axis=1)
        residual = residual + lax.psum(moe_part, "tensor")
        kept_act = pre_act
        saved.append(
            (
                normed_bf,
                norm_pull,
                head_view,
                log_total,
                mixed_rows,
                moe_bf,
                moe_pull,
                gate_probs,
                route_ids,
                slot_rows,
                picked,
                received,
                kept_act,
                chosen,
            )
        )
    mixed_out = residual.astype(jnp.bfloat16)
    upstream = cotangent.astype(jnp.float32)
    raw_grads = [None] * layer_count
    labels = lax.broadcasted_iota(jnp.int32, (1, 1, expert_count), 2)
    for layer_index in reversed(range(layer_count)):
        (
            normed_bf,
            norm_pull,
            head_view,
            log_total,
            mixed_rows,
            moe_bf,
            moe_pull,
            gate_probs,
            route_ids,
            slot_rows,
            picked,
            received,
            kept_act,
            chosen,
        ) = saved[layer_index]
        slot_grad = (
            (picked[:, :, None] * upstream[:, None, :])
            .astype(jnp.bfloat16)
            .reshape(-1, model_width)
        )
        grad_send = jnp.zeros((expert_count * capacity, model_width), jnp.bfloat16)
        grad_send = (
            grad_send.at[slot_rows].set(slot_grad).reshape(expert_count, capacity, model_width)
        )
        grad_recv = lax.all_to_all(grad_send, "expert", split_axis=0, concat_axis=0, tiled=True)
        source_count = grad_recv.shape[0]
        grad_recv = grad_recv.reshape(-1, model_width)
        flat_in = received.reshape(-1, model_width)
        pre_act = kept_act
        activation, gelu_pull = jax.vjp(jax.nn.gelu, pre_act)
        act_grad = jnp.einsum(
            "sd,fd->sf", grad_recv, expert_out[layer_index, 0], preferred_element_type=jnp.float32
        )
        pre_grad = gelu_pull(act_grad)[0].astype(jnp.bfloat16)
        grad_w_out = jnp.einsum(
            "sf,sd->fd",
            activation.astype(jnp.bfloat16),
            grad_recv,
            preferred_element_type=jnp.float32,
        )
        grad_w_in = jnp.einsum("sd,sf->df", flat_in, pre_grad, preferred_element_type=jnp.float32)
        input_grad = jnp.einsum(
            "sf,df->sd", pre_grad, expert_in[layer_index, 0], preferred_element_type=jnp.float32
        )
        input_grad = input_grad.reshape(source_count, capacity, model_width)
        home_grad = lax.all_to_all(input_grad, "expert", split_axis=0, concat_axis=0, tiled=True)
        row_grad = jnp.sum(
            home_grad.reshape(-1, model_width)[slot_rows].reshape(row_count, 2, model_width), axis=1
        )
        gate_dot = jnp.sum(upstream[:, None, :] * chosen, axis=-1)
        row_grad, gate_dot = lax.psum((row_grad, gate_dot), "tensor")
        prob_grad = jnp.sum(
            gate_dot[:, :, None] * (route_ids[:, :, None] == labels).astype(jnp.float32), axis=1
        )
        logit_grad = gate_probs * (
            prob_grad - jnp.sum(prob_grad * gate_probs, axis=-1, keepdims=True)
        )
        logit_grad = logit_grad.astype(jnp.bfloat16)
        grad_router = jnp.einsum(
            "td,te->de", moe_bf, logit_grad, preferred_element_type=jnp.float32
        )
        norm_grad = row_grad + jnp.einsum(
            "te,de->td", logit_grad, router[layer_index], preferred_element_type=jnp.float32
        )
        resid_grad, gain_two = moe_pull(norm_grad)
        upstream = upstream + resid_grad
        out_grad = upstream.astype(jnp.bfloat16)
        grad_attn_out = jnp.einsum(
            "tf,td->fd", mixed_rows, out_grad, preferred_element_type=jnp.float32
        )
        mixed_grad = jnp.einsum(
            "td,fd->tf", out_grad, attn_out[layer_index], preferred_element_type=jnp.float32
        )
        mixed_grad = mixed_grad.astype(jnp.bfloat16).reshape(
            image_count, SEQ, local_heads, HEAD_DIM
        )
        scores = (
            jnp.einsum(
                "bqhe,bkhe->bhqk", head_view[0], head_view[1], preferred_element_type=jnp.float32
            )
            * score_scale
        )
        attn_probs = jnp.exp(scores - log_total)
        value_grad = jnp.einsum(
            "bhqk,bqhe->bkhe",
            attn_probs.astype(jnp.bfloat16),
            mixed_grad,
            preferred_element_type=jnp.float32,
        )
        prob_grad = jnp.einsum(
            "bqhe,bkhe->bhqk", mixed_grad, head_view[2], preferred_element_type=jnp.float32
        )
        score_grad = attn_probs * (
            prob_grad - jnp.sum(prob_grad * attn_probs, axis=-1, keepdims=True)
        )
        score_grad = score_grad.astype(jnp.bfloat16)
        query_grad = (
            jnp.einsum(
                "bhqk,bkhe->bqhe", score_grad, head_view[1], preferred_element_type=jnp.float32
            )
            * score_scale
        )
        key_grad = (
            jnp.einsum(
                "bhqk,bqhe->bkhe", score_grad, head_view[0], preferred_element_type=jnp.float32
            )
            * score_scale
        )
        proj_grad = (
            jnp.stack([query_grad, key_grad, value_grad])
            .reshape(3, row_count, local_width)
            .astype(jnp.bfloat16)
        )
        grad_qkv = jnp.einsum(
            "td,ctf->cdf", normed_bf, proj_grad, preferred_element_type=jnp.float32
        )
        norm_grad = jnp.einsum(
            "ctf,cdf->td", proj_grad, attn_qkv[layer_index], preferred_element_type=jnp.float32
        )
        norm_grad = lax.psum(norm_grad, "tensor")
        resid_grad, gain_one = norm_pull(norm_grad)
        upstream = upstream + resid_grad
        gain_pair = jnp.stack([gain_one, gain_two])
        raw_grads[layer_index] = (
            grad_w_in,
            grad_w_out,
            grad_qkv,
            grad_attn_out,
            grad_router,
            gain_pair,
        )
    stacked = [jnp.stack([item[position] for item in raw_grads]) for position in range(6)]
    grad_in_all, grad_out_all = (
        lax.psum_scatter(stacked[0], "replica", scatter_dimension=1, tiled=True),
        lax.psum_scatter(stacked[1], "replica", scatter_dimension=2, tiled=True),
    )
    grad_qkv_all, grad_proj_all, grad_router_all, grad_gain_all = lax.psum(
        (stacked[2], stacked[3], stacked[4], stacked[5]), ("expert", "replica")
    )
    return (
        mixed_out,
        upstream,
        grad_gain_all,
        grad_qkv_all,
        grad_proj_all,
        grad_router_all,
        grad_in_all[:, None],
        grad_out_all[:, None],
    )


def solution(mesh):
    return jax.shard_map(
        on_device,
        mesh=mesh,
        in_specs=(
            P(("expert", "replica"), None),
            P(),
            P(None, None, None, "tensor"),
            P(None, "tensor", None),
            P(),
            P(None, "expert", None, "tensor"),
            P(None, "expert", "tensor", None),
            P(None, ("expert", "replica"), None),
            P(("expert", "replica"), None),
        ),
        out_specs=(
            P(("expert", "replica"), None),
            P(("expert", "replica"), None),
            P(),
            P(None, None, None, "tensor"),
            P(None, "tensor", None),
            P(),
            P(None, "expert", "replica", "tensor"),
            P(None, "expert", "tensor", "replica"),
        ),
        check_vma=False,
    )
```

profile of v0, /device:TPU:0, one launch (start us, length us, event | category | flops | bytes accessed | tf_op | source)
XLA Modules:
  0.0 1209.6 jit_solution(15359523138905654827)
XLA Ops:
  33.1 35.5 %all-reduce.14.cloned.1.call-done = f32[394,768]{1,0:T(8,128)} async-done(((f32[394,768]{1,0:T(8,128)}), f32[394,768]{1,0:T(8,128)}) %all-reduce.14.cloned.1.call-update) | async-done | bytes 1210384 | tf_op jit(solution)/shard_map/psum | solution.py:59
  79.4 42.6 %all_to_all.40 = bf16[8,128,768]{2,1,0:T(8,128)(2,1)S(1)} all-to-all(bf16[8,128,768]{2,1,0:T(8,128)(2,1)S(1)} %bitcast.271), channel_id=1, replica_groups=mesh['tensor'=2,'expert'=8,'replica'=2] {'expert'}, dimensions={0} | all-to-all | bytes 3145728 | tf_op jit(solution)/shard_map/all_to_all | solution.py:74
  150.6 57.4 %all-to-all-done.1 = f32[8,128,768]{2,1,0:T(8,128)S(1)} async-done(((f32[8,128,768]{2,1,0:T(8,128)}), f32[8,128,768]{2,1,0:T(8,128)S(1)}, u32[]{:S(2)}, u32[]{:S(2)}) %all-to-all-start.1) | async-done | bytes 3145760 | tf_op jit(solution)/shard_map/all_to_all | solution.py:83
  221.5 41.1 %all-reduce.16.cloned.1.call-done = f32[394,768]{1,0:T(8,128)} async-done(((f32[394,768]{1,0:T(8,128)}), f32[394,768]{1,0:T(8,128)}) %all-reduce.16.cloned.1.call-update) | async-done | bytes 1210384 | tf_op jit(solution)/shard_map/psum | solution.py:86
  288.3 33.4 %all-reduce.18.cloned.1.call-done = f32[394,768]{1,0:T(8,128)} async-done(((f32[394,768]{1,0:T(8,128)}), f32[394,768]{1,0:T(8,128)}) %all-reduce.18.cloned.1.call-update) | async-done | bytes 1210384 | tf_op jit(solution)/shard_map/psum | solution.py:59
  355.0 10.8 scatter_custom_fusion.2
  365.7 11.1 all-to-all-done.2
  388.9 29.1 %all-to-all-done.4 = bf16[8,128,768]{2,1,0:T(8,128)(2,1)} async-done(((bf16[8,128,768]{2,1,0:T(8,128)(2,1)}), bf16[8,128,768]{2,1,0:T(8,128)(2,1)}, u32[]{:S(2)}, u32[]{:S(2)}) %all-to-all-start.4) | async-done | bytes 1572896 | tf_op jit(solution)/shard_map/all_to_all | solution.py:136
  418.0 8.5 fusion.13
  443.0 64.0 %all-to-all-done.5 = f32[8,128,768]{2,1,0:T(8,128)S(1)} async-done(((f32[8,128,768]{2,1,0:T(8,128)}), f32[8,128,768]{2,1,0:T(8,128)S(1)}, u32[]{:S(2)}, u32[]{:S(2)}) %all-to-all-start.5) | async-done | bytes 3145760 | tf_op jit(solution)/shard_map/all_to_all | solution.py:157
  531.1 52.1 %all-to-all-done.3 = f32[8,128,768]{2,1,0:T(8,128)S(1)} async-done(((f32[8,128,768]{2,1,0:T(8,128)}), f32[8,128,768]{2,1,0:T(8,128)S(1)}, u32[]{:S(2)}, u32[]{:S(2)}) %all-to-all-start.3) | async-done | bytes 3145760 | tf_op jit(solution)/shard_map/all_to_all | solution.py:83
  599.2 9.9 psum.103
  629.0 42.9 %all-reduce.22.cloned.1.call-done = f32[394,768]{1,0:T(8,128)} async-done(((f32[394,768]{1,0:T(8,128)}), f32[394,768]{1,0:T(8,128)}) %all-reduce.22.cloned.1.call-update) | async-done | bytes 1210384 | tf_op jit(solution)/shard_map/psum | solution.py:231
  681.9 8.9 scatter_custom_fusion.3
  690.8 42.5 %all_to_all.41 = bf16[8,128,768]{2,1,0:T(8,128)(2,1)S(1)} all-to-all(bf16[8,128,768]{2,1,0:T(8,128)(2,1)} %bitcast.270), channel_id=1, replica_groups=mesh['tensor'=2,'expert'=8,'replica'=2] {'expert'}, dimensions={0} | all-to-all | bytes 3145728 | tf_op jit(solution)/shard_map/all_to_all | solution.py:136
  733.3 9.1 fusion.6
  745.1 74.1 %all_to_all.42 = f32[8,128,768]{2,1,0:T(8,128)S(1)} all-to-all(f32[8,128,768]{2,1,0:T(8,128)S(1)} %fusion.14), channel_id=1, replica_groups=mesh['tensor'=2,'expert'=8,'replica'=2] {'expert'}, dimensions={0} | all-to-all | bytes 6291456 | tf_op jit(solution)/shard_map/all_to_all | solution.py:157
  836.0 14.5 %psum.106 = f32[394,2]{1,0:T(8,128)S(1)} all-reduce(f32[394,2]{1,0:T(8,128)S(1)} %multiply_reduce_fusion.2), channel_id=1, replica_groups=mesh['tensor'=2,'expert'=8,'replica'=2] {'tensor'}, use_global_device_ids=true, to_apply=%region_47.50 | all-reduce | flops 788 | bytes 6304 | tf_op jit(solution)/shard_map/psum | solution.py:162
  850.8 27.6 %all-reduce.24.cloned.1.call-done = f32[394,768]{1,0:T(8,128)} async-done(((f32[394,768]{1,0:T(8,128)}), f32[394,768]{1,0:T(8,128)}) %all-reduce.24.cloned.1.call-update) | async-done | bytes 1210384 | tf_op jit(solution)/shard_map/psum | solution.py:162
  935.3 32.9 %all-reduce.28.cloned.1.call-done = (f32[394,768]{1,0:T(8,128)}, f32[394,768]{1,0:T(8,128)}) async-done(((f32[394,768]{1,0:T(8,128)}, f32[394,768]{1,0:T(8,128)}), (f32[394,768]{1,0:T(8,128)}, f32[394,768]{1,0:T(8,128)})) %all-reduce.28.cloned.1.call-update) | async-done | bytes 2420752 | tf_op jit(solution)/shard_map/psum | solution.py:86
  970.7 65.3 %all-reduce.2 = (f32[2,2,768]{2,1,0:T(2,128)}, f32[2,768,8]{1,2,0:T(8,128)}) all-reduce(f32[2,2,768]{2,1,0:T(2,128)S(1)} %pad_maximum_fusion.5, f32[2,768,8]{1,2,0:T(8,128)S(1)} %pad_maximum_fusion.4), channel_id=1, replica_groups=mesh['tensor'=2,'expert'=8,'replica'=2] {'expert','replica'}, use_global_device_ids=true, to_apply=%region_60.63 | all-reduce | flops 15360 | bytes 122880 | tf_op jit(solution)/shard_map/psum | solution.py:248
  1039.5 118.8 %all-reduce.26.cloned.1.call-done = (f32[2,3,768,384]{2,3,1,0:T(8,128)}, f32[2,384,768]{2,1,0:T(8,128)}) async-done(((f32[2,3,768,384]{2,3,1,0:T(8,128)}, f32[2,384,768]{2,1,0:T(8,128)}), (f32[2,3,768,384]{2,3,1,0:T(8,128)}, f32[2,384,768]{2,1,0:T(8,128)})) %all-reduce.26.cloned.1.call-update) | async-done | bytes 9437200 | tf_op jit(solution)/shard_map/psum | solution.py:248
  1166.5 12.7 %reduce-scatter.5.cloned.1.call-done = f32[2,1536,384]{2,1,0:T(8,128)} async-done(((f32[2,1536,768]{2,1,0:T(8,128)}), f32[2,1536,384]{2,1,0:T(8,128)}) %reduce-scatter.5.cloned.1.call-update) | async-done | bytes 4718608 | tf_op jit(solution)/shard_map/reduce_scatter | solution.py:246
  1179.1 22.0 %reduce-scatter.3.cloned.1.call-done = f32[2,384,1536]{2,1,0:T(8,128)} async-done(((f32[2,768,1536]{2,1,0:T(8,128)}), f32[2,384,1536]{2,1,0:T(8,128)}) %reduce-scatter.3.cloned.1.call-update) | async-done | bytes 4718608 | tf_op jit(solution)/shard_map/reduce_scatter | solution.py:245
  (499 shorter events, 326.6 us)
Async XLA Ops:
  7.2 61.4 %all-reduce.14.cloned.1.call-start = ((), (), s32[]{:S(2)}) async-start(), calls=%async_computation.10 | async-start | bytes 2457600 | tf_op jit(solution)/shard_map/psum | solution.py:59
  11.3 59.1 %copy-start.85 = (f32[768]{0:T(1024)}, f32[768]{0:T(1024)S(1)}, u32[]{:S(2)}) copy-start(f32[768]{0:T(1024)S(1)} %get-tuple-element.61) | copy-start | bytes 9220
  33.1 104.6 %copy-start.116 = (s32[788]{0:T(1024)}, s32[788]{0:T(1024)S(1)}, u32[]{:S(2)}) copy-start(s32[788]{0:T(1024)S(1)} %fusion.150) | copy-start | bytes 9460
  79.4 50.2 %slice-start = ((s8[4718592]{0:T(1024)(128)(4,1)}), s8[4194304]{0:T(1024)(128)(4,1)S(1)}, s32[]{:S(2)}) async-start(s8[4718592]{0:T(1024)(128)(4,1)} %bitcast.280), calls=%async_computation.20 | async-start | bytes 8388608
  133.9 74.1 %all-to-all-start.1 = ((f32[8,128,768]{2,1,0:T(8,128)}), f32[8,128,768]{2,1,0:T(8,128)S(1)}, u32[]{:S(2)}, u32[]{:S(2)}) async-start(f32[8,128,768]{2,1,0:T(8,128)} %fusion.20), calls=%async_computation.1 | async-start | bytes 6291456 | tf_op jit(solution)/shard_map/all_to_all | solution.py:83
  137.7 124.9 %all-reduce.16.cloned.1.call-start = ((), (), s32[]{:S(2)}) async-start(), calls=%async_computation.11 | async-start | bytes 2457600 | tf_op jit(solution)/shard_map/psum | solution.py:86
  137.7 70.2 %copy-start.100 = (s32[1024]{0:T(1024)}, s32[1024]{0:T(1024)S(1)}, u32[]{:S(2)}) copy-start(s32[1024]{0:T(1024)S(1)} %pad_clamp_fusion.1) | copy-start | bytes 12292
  220.3 101.4 %all-reduce.18.cloned.1.call-start = ((), (), s32[]{:S(2)}) async-start(), calls=%async_computation.12 | async-start | bytes 2457600 | tf_op jit(solution)/shard_map/psum | solution.py:59
  264.2 57.4 %copy-start.11 = (f32[394,768]{1,0:T(8,128)}, f32[394,768]{1,0:T(8,128)S(1)}, u32[]{:S(2)}) copy-start(f32[394,768]{1,0:T(8,128)S(1)} %get-tuple-element.79) | copy-start | bytes 3631108
  334.1 42.8 %all-to-all-start.2 = ((bf16[8,128,768]{2,1,0:T(8,128)(2,1)}), bf16[8,128,768]{2,1,0:T(8,128)(2,1)S(1)}, u32[]{:S(2)}, u32[]{:S(2)}) async-start(bf16[8,128,768]{2,1,0:T(8,128)(2,1)} %bitcast.268), calls=%async_computation.2 | async-start | bytes 3145728 | tf_op jit(solution)/shard_map/all_to_all | solution.py:74
  376.9 41.2 %all-to-all-start.4 = ((bf16[8,128,768]{2,1,0:T(8,128)(2,1)}), bf16[8,128,768]{2,1,0:T(8,128)(2,1)}, u32[]{:S(2)}, u32[]{:S(2)}) async-start(bf16[8,128,768]{2,1,0:T(8,128)(2,1)} %bitcast.269), calls=%async_computation.4 | async-start | bytes 3145728 | tf_op jit(solution)/shard_map/all_to_all | solution.py:136
  432.5 74.5 %all-to-all-start.5 = ((f32[8,128,768]{2,1,0:T(8,128)}), f32[8,128,768]{2,1,0:T(8,128)S(1)}, u32[]{:S(2)}, u32[]{:S(2)}) async-start(f32[8,128,768]{2,1,0:T(8,128)} %fusion.16), calls=%async_computation.5 | async-start | bytes 6291456 | tf_op jit(solution)/shard_map/all_to_all | solution.py:157
  508.7 74.5 %all-to-all-start.3 = ((f32[8,128,768]{2,1,0:T(8,128)}), f32[8,128,768]{2,1,0:T(8,128)S(1)}, u32[]{:S(2)}, u32[]{:S(2)}) async-start(f32[8,128,768]{2,1,0:T(8,128)} %fusion.18), calls=%async_computation.3 | async-start | bytes 6291456 | tf_op jit(solution)/shard_map/all_to_all | solution.py:83
  512.3 97.0 %all-reduce.20.cloned.1.call-start = ((), (), s32[]{:S(2)}) async-start(), calls=%async_computation.13 | async-start | bytes 2457600 | tf_op jit(solution)/shard_map/psum | solution.py:162
  528.9 143.0 %all-reduce.22.cloned.1.call-start = ((), (), s32[]{:S(2)}) async-start(), calls=%async_computation.14 | async-start | bytes 2457600 | tf_op jit(solution)/shard_map/psum | solution.py:231
  625.0 46.9 %copy-start.103 = (f32[394]{0:T(512)S(1)}, f32[394]{0:T(512)}, u32[]{:S(2)}) copy-start(f32[394]{0:T(512)} %copy-done.102) | copy-start | bytes 4732
  628.6 249.8 %all-reduce.24.cloned.1.call-start = ((), (), s32[]{:S(2)}) async-start(), calls=%async_computation.15 | async-start | bytes 2457600 | tf_op jit(solution)/shard_map/psum | solution.py:162
  681.9 60.6 %slice-start.4 = ((s8[4718592]{0:T(1024)(128)(4,1)}), s8[524288]{0:T(1024)(128)(4,1)S(1)}, s32[]{:S(2)}) async-start(s8[4718592]{0:T(1024)(128)(4,1)} %bitcast.284), calls=%async_computation.24 | async-start | bytes 1048576
  745.1 74.1 %copy-start.101 = (s32[1024]{0:T(1024)S(1)}, s32[1024]{0:T(1024)}, u32[]{:S(2)}) copy-start(s32[1024]{0:T(1024)} %copy-done.100) | copy-start | bytes 12292
  832.7 135.4 %all-reduce.28.cloned.1.call-start = ((), (), s32[]{:S(2)}) async-start(), calls=%async_computation.19 | async-start | bytes 4915200 | tf_op jit(solution)/shard_map/psum | solution.py:86
  897.1 261.2 %all-reduce.26.cloned.1.call-start = ((), (), s32[]{:S(2)}) async-start(), calls=%async_computation.18 | async-start | bytes 18874368 | tf_op jit(solution)/shard_map/psum | solution.py:248
  908.8 270.3 %reduce-scatter.5.cloned.1.call-start = ((), (), s32[]{:S(2)}) async-start(), calls=%async_computation.17 | async-start | bytes 14155776 | tf_op jit(solution)/shard_map/reduce_scatter | solution.py:246
  921.2 280.0 %reduce-scatter.3.cloned.1.call-start = ((), (), s32[]{:S(2)}) async-start(), calls=%async_computation.16 | async-start | bytes 14155776 | tf_op jit(solution)/shard_map/reduce_scatter | solution.py:245
  968.2 67.8 %copy-start.7 = (f32[394,768]{1,0:T(8,128)S(1)}, f32[394,768]{1,0:T(8,128)}, u32[]{:S(2)}) copy-start(f32[394,768]{1,0:T(8,128)} %copy-done.5) | copy-start | bytes 3631108
  (118 other events, 1070.1 us)
Sparse Core Ops, SparseCore 0:
  21.9 46.6 all-reduce.13
  220.4 42.0 all-reduce.15
  277.6 43.9 all-reduce.17
  529.0 44.3 all-reduce.19
  628.7 43.1 all-reduce.21
  832.9 45.4 all-reduce.23
  897.2 70.9 all-reduce.27
  972.5 185.7 all-reduce.25
  1161.2 17.8 reduce-scatter.4
  1181.9 19.1 reduce-scatter.2
where the time goes:
time: 1220 us; the launch traced here: 1210 us
  waiting for transfers between devices  581 us (48%)
  blocking collectives  249 us (20%)
  local copies, waits for them, and re-layouts  154 us (13%)
  matrix products  98.9 us (8%)
  other arithmetic  88.1 us (7%)
  starting transfers between devices  22.7 us (2%)
  between operations  16.4 us (1%)
    psum x1, waiting for transfers between devices, on_device(): lax.psum((stacked[2], stacked[3], stacked[4], stacked[5]), ('expert', 're...  119 us
    all_to_all x2, waiting for transfers between devices, on_device(): lax.all_to_all(expert_part, 'expert', split_axis=0, concat_axis=0, tiled=...  109 us
    all_to_all x1, blocking collectives, on_device(): lax.all_to_all(input_grad, 'expert', split_axis=0, concat_axis=0, tiled=T...  74.1 us
    psum x2, waiting for transfers between devices, on_device(): residual = residual + lax.psum(moe_part, 'tensor')  74 us
    psum x2, waiting for transfers between devices, on_device(): residual = residual + lax.psum(attn_part, 'tensor')  68.9 us
    psum x1, blocking collectives, on_device(): lax.psum((stacked[2], stacked[3], stacked[4], stacked[5]), ('expert', 're...  65.3 us
    all_to_all x1, waiting for transfers between devices, on_device(): lax.all_to_all(input_grad, 'expert', split_axis=0, concat_axis=0, tiled=T...  64 us
    psum x1, waiting for transfers between devices, on_device(): norm_grad = lax.psum(norm_grad, 'tensor')  42.9 us
  transfers between devices with their start and end apart: 15, of which 14 were waited for; matrix products, arithmetic and copies ran while one was open for 13% of the time, Pallas kernels for 0%

commit v1 on v0

--- a/solution.py
+++ b/solution.py
@@ -246,7 +246,7 @@
         lax.psum_scatter(stacked[1], "replica", scatter_dimension=2, tiled=True),
     )
     grad_qkv_all, grad_proj_all, grad_router_all, grad_gain_all = lax.psum(
-        (stacked[2], stacked[3], stacked[4], stacked[5]), ("expert", "replica")
+        lax.psum((stacked[2], stacked[3], stacked[4], stacked[5]), "replica"), "expert"
     )
     return (
         mixed_out,

time: 1220 us -> 1390 us (1.14)
  waiting for transfers between devices: 581 us -> 835 us
  blocking collectives: 249 us -> 154 us
    psum x1 -> x2, waiting for transfers between devices: 119 us -> 291 us  [the longest x1 254 us: on_device(): lax.psum(lax.psum((stacked[2], stacked[3], stacked[4], stacked[5]), 'repl...]
    all_to_all x1 -> x0, blocking collectives: 74.1 us -> none  [on_device(): lax.all_to_all(input_grad, 'expert', split_axis=0, concat_axis=0, tiled=T...]
    all_to_all x1 -> x2, waiting for transfers between devices: 64 us -> 134 us  [on_device(): lax.all_to_all(input_grad, 'expert', split_axis=0, concat_axis=0, tiled=T...]
    psum x1 -> x2, blocking collectives: 65.3 us -> 44.5 us  [the longest x1 40.9 us: on_device(): lax.psum(lax.psum((stacked[2], stacked[3], stacked[4], stacked[5]), 'repl...]
    psum x2, waiting for transfers between devices: 74 us -> 88.6 us  [on_device(): residual = residual + lax.psum(moe_part, 'tensor')]
    unnamed x262 -> x266, local copies, waits for them, and re-layouts: 32.4 us -> 33.8 us
  transfers between devices with their start and end apart: 15 -> 17, of which waited for: 14 -> 16; matrix products, arithmetic and copies ran while one was open for 13% -> 11% of each run, Pallas kernels for 0% -> 0%
where the time goes in v1:
time: 1390 us; the launch traced here: 1380 us
  waiting for transfers between devices  835 us (60%)
  local copies, waits for them, and re-layouts  156 us (11%)
  blocking collectives  154 us (11%)
  matrix products  104 us (7%)
  other arithmetic  86.5 us (6%)
  starting transfers between devices  26.5 us (2%)
  between operations  16 us (1%)
    psum x1, waiting for transfers between devices, on_device(): lax.psum(lax.psum((stacked[2], stacked[3], stacked[4], stacked[5]), 'repl...  254 us
    all_to_all x2, waiting for transfers between devices, on_device(): lax.all_to_all(input_grad, 'expert', split_axis=0, concat_axis=0, tiled=T...  134 us
    all_to_all x2, waiting for transfers between devices, on_device(): lax.all_to_all(expert_part, 'expert', split_axis=0, concat_axis=0, tiled=...  109 us
    psum x2, waiting for transfers between devices, on_device(): residual = residual + lax.psum(moe_part, 'tensor')  88.6 us
    psum x2, waiting for transfers between devices, on_device(): residual = residual + lax.psum(attn_part, 'tensor')  68.9 us
    psum x1, waiting for transfers between devices, on_device(): norm_grad = lax.psum(norm_grad, 'tensor')  43.2 us
    all_to_all x1, blocking collectives, on_device(): lax.all_to_all(send_buffer, 'expert', split_axis=0, concat_axis=0, tiled=...  42.6 us
    all_to_all x1, blocking collectives, on_device(): lax.all_to_all(grad_send, 'expert', split_axis=0, concat_axis=0, tiled=True)  42.5 us
  transfers between devices with their start and end apart: 17, of which 16 were waited for; matrix products, arithmetic and copies ran while one was open for 11% of the time, Pallas kernels for 0%

profile of v1, /device:TPU:0, one launch (start us, length us, event | category | flops | bytes accessed | tf_op | source)
XLA Modules:
  0.0 1377.2 jit_solution(8304651946528401076)
XLA Ops:
  33.0 35.5 %all-reduce.17.cloned.1.call-done = f32[394,768]{1,0:T(8,128)} async-done(((f32[394,768]{1,0:T(8,128)}), f32[394,768]{1,0:T(8,128)}) %all-reduce.17.cloned.1.call-update) | async-done | bytes 1210384 | tf_op jit(solution)/shard_map/psum | solution.py:59
  79.4 42.6 %all_to_all.40 = bf16[8,128,768]{2,1,0:T(8,128)(2,1)S(1)} all-to-all(bf16[8,128,768]{2,1,0:T(8,128)(2,1)S(1)} %bitcast.271), channel_id=1, replica_groups=mesh['tensor'=2,'expert'=8,'replica'=2] {'expert'}, dimensions={0} | all-to-all | bytes 3145728 | tf_op jit(solution)/shard_map/all_to_all | solution.py:74
  150.6 57.3 %all-to-all-done.1 = f32[8,128,768]{2,1,0:T(8,128)S(1)} async-done(((f32[8,128,768]{2,1,0:T(8,128)}), f32[8,128,768]{2,1,0:T(8,128)S(1)}, u32[]{:S(2)}, u32[]{:S(2)}) %all-to-all-start.1) | async-done | bytes 3145760 | tf_op jit(solution)/shard_map/all_to_all | solution.py:83
  221.4 41.1 %all-reduce.19.cloned.1.call-done = f32[394,768]{1,0:T(8,128)} async-done(((f32[394,768]{1,0:T(8,128)}), f32[394,768]{1,0:T(8,128)}) %all-reduce.19.cloned.1.call-update) | async-done | bytes 1210384 | tf_op jit(solution)/shard_map/psum | solution.py:86
  288.2 33.4 %all-reduce.21.cloned.1.call-done = f32[394,768]{1,0:T(8,128)} async-done(((f32[394,768]{1,0:T(8,128)}), f32[394,768]{1,0:T(8,128)}) %all-reduce.21.cloned.1.call-update) | async-done | bytes 1210384 | tf_op jit(solution)/shard_map/psum | solution.py:59
  354.9 10.8 scatter_custom_fusion.2
  365.7 11.1 all-to-all-done.2
  388.8 29.2 %all-to-all-done.4 = bf16[8,128,768]{2,1,0:T(8,128)(2,1)} async-done(((bf16[8,128,768]{2,1,0:T(8,128)(2,1)}), bf16[8,128,768]{2,1,0:T(8,128)(2,1)}, u32[]{:S(2)}, u32[]{:S(2)}) %all-to-all-start.4) | async-done | bytes 1572896 | tf_op jit(solution)/shard_map/all_to_all | solution.py:136
  443.0 64.0 %all-to-all-done.5 = f32[8,128,768]{2,1,0:T(8,128)S(1)} async-done(((f32[8,128,768]{2,1,0:T(8,128)}), f32[8,128,768]{2,1,0:T(8,128)S(1)}, u32[]{:S(2)}, u32[]{:S(2)}) %all-to-all-start.5) | async-done | bytes 3145760 | tf_op jit(solution)/shard_map/all_to_all | solution.py:157
  531.0 52.1 %all-to-all-done.3 = f32[8,128,768]{2,1,0:T(8,128)S(1)} async-done(((f32[8,128,768]{2,1,0:T(8,128)}), f32[8,128,768]{2,1,0:T(8,128)S(1)}, u32[]{:S(2)}, u32[]{:S(2)}) %all-to-all-start.3) | async-done | bytes 3145760 | tf_op jit(solution)/shard_map/all_to_all | solution.py:83
  599.2 9.8 psum.131
  628.7 43.2 %all-reduce.25.cloned.1.call-done = f32[394,768]{1,0:T(8,128)} async-done(((f32[394,768]{1,0:T(8,128)}), f32[394,768]{1,0:T(8,128)}) %all-reduce.25.cloned.1.call-update) | async-done | bytes 1210384 | tf_op jit(solution)/shard_map/psum | solution.py:231
  682.1 8.9 scatter_custom_fusion.3
  691.0 42.5 %all_to_all.41 = bf16[8,128,768]{2,1,0:T(8,128)(2,1)S(1)} all-to-all(bf16[8,128,768]{2,1,0:T(8,128)(2,1)} %bitcast.270), channel_id=1, replica_groups=mesh['tensor'=2,'expert'=8,'replica'=2] {'expert'}, dimensions={0} | all-to-all | bytes 3145728 | tf_op jit(solution)/shard_map/all_to_all | solution.py:136
  733.5 9.1 fusion.6
  752.5 70.2 %all-to-all-done.7 = f32[8,128,768]{2,1,0:T(8,128)S(1)} async-done(((f32[8,128,768]{2,1,0:T(8,128)}), f32[8,128,768]{2,1,0:T(8,128)S(1)}, u32[]{:S(2)}, u32[]{:S(2)}) %all-to-all-start.7) | async-done | bytes 3145760 | tf_op jit(solution)/shard_map/all_to_all | solution.py:157
  842.7 14.4 %psum.134 = f32[394,2]{1,0:T(8,128)S(1)} all-reduce(f32[394,2]{1,0:T(8,128)S(1)} %multiply_reduce_fusion.2), channel_id=1, replica_groups=mesh['tensor'=2,'expert'=8,'replica'=2] {'tensor'}, use_global_device_ids=true, to_apply=%region_47.50 | all-reduce | flops 788 | bytes 6304 | tf_op jit(solution)/shard_map/psum | solution.py:162
  857.3 25.8 %all-reduce.27.cloned.1.call-done = f32[394,768]{1,0:T(8,128)} async-done(((f32[394,768]{1,0:T(8,128)}), f32[394,768]{1,0:T(8,128)}) %all-reduce.27.cloned.1.call-update) | async-done | bytes 1210384 | tf_op jit(solution)/shard_map/psum | solution.py:162
  911.8 37.3 %all-reduce.31.cloned.1.call-done = (f32[2,3,768,384]{2,3,1,0:T(8,128)}, f32[2,384,768]{2,1,0:T(8,128)}) async-done(((f32[2,3,768,384]{2,3,1,0:T(8,128)}, f32[2,384,768]{2,1,0:T(8,128)}), (f32[2,3,768,384]{2,3,1,0:T(8,128)}, f32[2,384,768]{2,1,0:T(8,128)})) %all-reduce.31.cloned.1.call-update) | async-done | bytes 9437200 | tf_op jit(solution)/shard_map/psum | solution.py:249
  976.1 47.6 %all-reduce.33.cloned.1.call-done = (f32[394,768]{1,0:T(8,128)}, f32[394,768]{1,0:T(8,128)}) async-done(((f32[394,768]{1,0:T(8,128)}, f32[394,768]{1,0:T(8,128)}), (f32[394,768]{1,0:T(8,128)}, f32[394,768]{1,0:T(8,128)})) %all-reduce.33.cloned.1.call-update) | async-done | bytes 2420752 | tf_op jit(solution)/shard_map/psum | solution.py:86
  1029.8 40.9 %all-reduce.2 = (f32[2,2,768]{2,1,0:T(2,128)}, f32[2,768,8]{1,2,0:T(8,128)}) all-reduce(f32[2,2,768]{2,1,0:T(2,128)S(1)} %get-tuple-element.68, f32[2,768,8]{1,2,0:T(8,128)S(1)} %get-tuple-element.69), channel_id=1, replica_groups=mesh['tensor'=2,'expert'=8,'replica'=2] {'expert'}, use_global_device_ids=true, to_apply=%region_61.64 | all-reduce | flops 15360 | bytes 122880 | tf_op jit(solution)/shard_map/psum | solution.py:248
  1074.1 253.6 %all-reduce.29.cloned.1.call-done = (f32[2,3,768,384]{2,3,1,0:T(8,128)}, f32[2,384,768]{2,1,0:T(8,128)}) async-done(((f32[2,3,768,384]{2,3,1,0:T(8,128)}, f32[2,384,768]{2,1,0:T(8,128)}), (f32[2,3,768,384]{2,3,1,0:T(8,128)}, f32[2,384,768]{2,1,0:T(8,128)})) %all-reduce.29.cloned.1.call-update) | async-done | bytes 9437200 | tf_op jit(solution)/shard_map/psum | solution.py:248
  1335.9 11.2 reduce-scatter.5.cloned.1.call-done
  1347.2 21.9 %reduce-scatter.3.cloned.1.call-done = f32[2,384,1536]{2,1,0:T(8,128)} async-done(((f32[2,768,1536]{2,1,0:T(8,128)}), f32[2,384,1536]{2,1,0:T(8,128)}) %reduce-scatter.3.cloned.1.call-update) | async-done | bytes 4718608 | tf_op jit(solution)/shard_map/reduce_scatter | solution.py:245
  (508 shorter events, 347.9 us)
Async XLA Ops:
  7.2 61.4 %all-reduce.17.cloned.1.call-start = ((), (), s32[]{:S(2)}) async-start(), calls=%async_computation.10 | async-start | bytes 2457600 | tf_op jit(solution)/shard_map/psum | solution.py:59
  11.3 59.1 %copy-start.85 = (f32[768]{0:T(1024)}, f32[768]{0:T(1024)S(1)}, u32[]{:S(2)}) copy-start(f32[768]{0:T(1024)S(1)} %get-tuple-element.61) | copy-start | bytes 9220
  33.0 104.6 %copy-start.118 = (s32[788]{0:T(1024)}, s32[788]{0:T(1024)S(1)}, u32[]{:S(2)}) copy-start(s32[788]{0:T(1024)S(1)} %fusion.150) | copy-start | bytes 9460
  79.4 50.2 %slice-start = ((s8[4718592]{0:T(1024)(128)(4,1)}), s8[4194304]{0:T(1024)(128)(4,1)S(1)}, s32[]{:S(2)}) async-start(s8[4718592]{0:T(1024)(128)(4,1)} %bitcast.280), calls=%async_computation.21 | async-start | bytes 8388608
  133.8 74.1 %all-to-all-start.1 = ((f32[8,128,768]{2,1,0:T(8,128)}), f32[8,128,768]{2,1,0:T(8,128)S(1)}, u32[]{:S(2)}, u32[]{:S(2)}) async-start(f32[8,128,768]{2,1,0:T(8,128)} %fusion.20), calls=%async_computation.1 | async-start | bytes 6291456 | tf_op jit(solution)/shard_map/all_to_all | solution.py:83
  137.6 124.8 %all-reduce.19.cloned.1.call-start = ((), (), s32[]{:S(2)}) async-start(), calls=%async_computation.11 | async-start | bytes 2457600 | tf_op jit(solution)/shard_map/psum | solution.py:86
  137.7 70.2 %copy-start.102 = (s32[1024]{0:T(1024)}, s32[1024]{0:T(1024)S(1)}, u32[]{:S(2)}) copy-start(s32[1024]{0:T(1024)S(1)} %pad_clamp_fusion.1) | copy-start | bytes 12292
  220.2 101.4 %all-reduce.21.cloned.1.call-start = ((), (), s32[]{:S(2)}) async-start(), calls=%async_computation.12 | async-start | bytes 2457600 | tf_op jit(solution)/shard_map/psum | solution.py:59
  264.1 57.5 %copy-start.11 = (f32[394,768]{1,0:T(8,128)}, f32[394,768]{1,0:T(8,128)S(1)}, u32[]{:S(2)}) copy-start(f32[394,768]{1,0:T(8,128)S(1)} %get-tuple-element.83) | copy-start | bytes 3631108
  334.0 42.8 %all-to-all-start.2 = ((bf16[8,128,768]{2,1,0:T(8,128)(2,1)}), bf16[8,128,768]{2,1,0:T(8,128)(2,1)S(1)}, u32[]{:S(2)}, u32[]{:S(2)}) async-start(bf16[8,128,768]{2,1,0:T(8,128)(2,1)} %bitcast.268), calls=%async_computation.2 | async-start | bytes 3145728 | tf_op jit(solution)/shard_map/all_to_all | solution.py:74
  376.8 41.2 %all-to-all-start.4 = ((bf16[8,128,768]{2,1,0:T(8,128)(2,1)}), bf16[8,128,768]{2,1,0:T(8,128)(2,1)}, u32[]{:S(2)}, u32[]{:S(2)}) async-start(bf16[8,128,768]{2,1,0:T(8,128)(2,1)} %bitcast.269), calls=%async_computation.4 | async-start | bytes 3145728 | tf_op jit(solution)/shard_map/all_to_all | solution.py:136
  432.4 74.5 %all-to-all-start.5 = ((f32[8,128,768]{2,1,0:T(8,128)}), f32[8,128,768]{2,1,0:T(8,128)S(1)}, u32[]{:S(2)}, u32[]{:S(2)}) async-start(f32[8,128,768]{2,1,0:T(8,128)} %fusion.16), calls=%async_computation.5 | async-start | bytes 6291456 | tf_op jit(solution)/shard_map/all_to_all | solution.py:157
  508.6 74.5 %all-to-all-start.3 = ((f32[8,128,768]{2,1,0:T(8,128)}), f32[8,128,768]{2,1,0:T(8,128)S(1)}, u32[]{:S(2)}, u32[]{:S(2)}) async-start(f32[8,128,768]{2,1,0:T(8,128)} %fusion.18), calls=%async_computation.3 | async-start | bytes 6291456 | tf_op jit(solution)/shard_map/all_to_all | solution.py:83
  512.2 97.0 %all-reduce.23.cloned.1.call-start = ((), (), s32[]{:S(2)}) async-start(), calls=%async_computation.13 | async-start | bytes 2457600 | tf_op jit(solution)/shard_map/psum | solution.py:162
  528.8 143.1 %all-reduce.25.cloned.1.call-start = ((), (), s32[]{:S(2)}) async-start(), calls=%async_computation.14 | async-start | bytes 2457600 | tf_op jit(solution)/shard_map/psum | solution.py:231
  682.1 62.2 %slice-start.4 = ((s8[4718592]{0:T(1024)(128)(4,1)}), s8[524288]{0:T(1024)(128)(4,1)S(1)}, s32[]{:S(2)}) async-start(s8[4718592]{0:T(1024)(128)(4,1)} %bitcast.284), calls=%async_computation.25 | async-start | bytes 1048576
  748.6 74.1 %copy-start.103 = (s32[1024]{0:T(1024)S(1)}, s32[1024]{0:T(1024)}, u32[]{:S(2)}) copy-start(s32[1024]{0:T(1024)} %copy-done.102) | copy-start | bytes 12292
  748.6 74.1 %all-to-all-start.7 = ((f32[8,128,768]{2,1,0:T(8,128)}), f32[8,128,768]{2,1,0:T(8,128)S(1)}, u32[]{:S(2)}, u32[]{:S(2)}) async-start(f32[8,128,768]{2,1,0:T(8,128)} %fusion.14), calls=%async_computation.7 | async-start | bytes 6291456 | tf_op jit(solution)/shard_map/all_to_all | solution.py:157
  752.4 130.7 %all-reduce.27.cloned.1.call-start = ((), (), s32[]{:S(2)}) async-start(), calls=%async_computation.15 | async-start | bytes 2457600 | tf_op jit(solution)/shard_map/psum | solution.py:162
  836.4 112.7 %all-reduce.31.cloned.1.call-start = ((), (), s32[]{:S(2)}) async-start(), calls=%async_computation.19 | async-start | bytes 18874368 | tf_op jit(solution)/shard_map/psum | solution.py:249
  908.2 115.5 %all-reduce.33.cloned.1.call-start = ((), (), s32[]{:S(2)}) async-start(), calls=%async_computation.20 | async-start | bytes 4915200 | tf_op jit(solution)/shard_map/psum | solution.py:86
  911.8 415.9 %all-reduce.29.cloned.1.call-start = ((), (), s32[]{:S(2)}) async-start(), calls=%async_computation.18 | async-start | bytes 18874368 | tf_op jit(solution)/shard_map/psum | solution.py:248
  949.2 398.0 %reduce-scatter.5.cloned.1.call-start = ((), (), s32[]{:S(2)}) async-start(), calls=%async_computation.17 | async-start | bytes 14155776 | tf_op jit(solution)/shard_map/reduce_scatter | solution.py:246
  962.0 407.1 %reduce-scatter.3.cloned.1.call-start = ((), (), s32[]{:S(2)}) async-start(), calls=%async_computation.16 | async-start | bytes 14155776 | tf_op jit(solution)/shard_map/reduce_scatter | solution.py:245
  (122 other events, 1205.5 us)
Sparse Core Ops, SparseCore 0:
  21.8 46.6 all-reduce.16
  220.3 42.0 all-reduce.18
  277.6 43.9 all-reduce.20
  528.9 44.3 all-reduce.22
  628.7 43.1 all-reduce.24
  836.6 46.4 all-reduce.26
  908.3 40.7 all-reduce.30
  951.5 72.1 all-reduce.32
  1027.7 299.8 all-reduce.28
  1330.4 16.7 reduce-scatter.4
  1350.0 19.0 reduce-scatter.2
